TPU v7x, 32 devices: a whole 2x2x4 slice. The times are simulated.
32 devices in a mesh: rep: 16 (over z, x, core), shard: 2 (over y).
Axes of the slice: x: 2, y: 2, z: 4, core: 2. Of those that a mesh axis runs over, the one named last changes fastest.
Arguments:
- tokens: bfloat16 [4096, 1024], P(('rep', 'shard')), may hold values from -6 to 6
- lengths: int32 [32], P(('rep', 'shard')), may hold values from 32 to 128, as said below
- qkv_weight: bfloat16 [1024, 3072], P('shard'), may hold values from -0.1875 to 0.1875
- query_bias: bfloat16 [1024], P('shard'), may hold values from -3 to 3
- value_bias: bfloat16 [1024], P('shard'), may hold values from -3 to 3
- proj_weight: bfloat16 [1024, 1024], P('shard'), may hold values from -0.5 to 0.5
- proj_bias: bfloat16 [1024], P('shard'), may hold values from -3 to 3
- attn_gain: bfloat16 [1024], P('shard'), may hold values from 0.5 to 1.5
- attn_shift: bfloat16 [1024], P('shard'), may hold values from -3 to 3
- up_weight: bfloat16 [1024, 4096], P('shard'), may hold values from -0.1875 to 0.1875
- up_bias: bfloat16 [4096], P('shard'), may hold values from -3 to 3
- down_weight: bfloat16 [4096, 1024], P('shard'), may hold values from -0.09375 to 0.09375
- down_bias: bfloat16 [1024], P('shard'), may hold values from -3 to 3
- ffn_gain: bfloat16 [1024], P('shard'), may hold values from 0.5 to 1.5
- ffn_shift: bfloat16 [1024], P('shard'), may hold values from -3 to 3
- cotangent: bfloat16 [4096, 1024], P(('rep', 'shard')), may hold values from -6 to 6
Outputs:
- layer_output: bfloat16 [4096, 1024], P(('rep', 'shard'))
- grad_tokens: bfloat16 [4096, 1024], P(('rep', 'shard'))
- grad_qkv_weight: float32 [1024, 3072], P('shard')
- grad_query_bias: float32 [1024], P('shard')
- grad_value_bias: float32 [1024], P('shard')
- grad_proj_weight: float32 [1024, 1024], P('shard')
- grad_proj_bias: float32 [1024], P('shard')
- grad_attn_gain: float32 [1024], P('shard')
- grad_attn_shift: float32 [1024], P('shard')
- grad_up_weight: float32 [1024, 4096], P('shard')
- grad_up_bias: float32 [4096], P('shard')
- grad_down_weight: float32 [4096, 1024], P('shard')
- grad_down_bias: float32 [1024], P('shard')
- grad_ffn_gain: float32 [1024], P('shard')
- grad_ffn_shift: float32 [1024], P('shard')
Inputs may be any that keep to these rules, and one draw needn't show every extreme that they name: `lengths`: every sequence has at least one quarter of its 128 tokens valid; some sequence is whole and some has exactly 32 valid tokens.
All inputs are finite; a program needn't handle non-finite values.
Results may differ from a plain program's by a relative error of at most 0.018.
Values may be sent and summed in bfloat16 or wider, within the bound.
No kernel may reach another device: no remote copies, remote signals or barrier semaphores. Data moves between devices by JAX's collectives and lax.ppermute only.
A program may use at most 192 MiB of HBM per device.

v0:
```python
import jax
import jax.numpy as jnp
from jax import lax
from jax.sharding import PartitionSpec as P

HEADS = 16
HEAD_DIM = 64
LEN = 128
EPSILON = 1e-05
SQRT_HALF = 0.7071067811865476
INV_ROOT_TAU = 0.3989422804014327


def gelu_value(pre_act):
    return 0.5 * pre_act * (1.0 + lax.erf(pre_act * SQRT_HALF))


def gelu_slope(pre_act):
    return 0.5 * (1.0 + lax.erf(pre_act * SQRT_HALF)) + pre_act * INV_ROOT_TAU * jnp.exp(
        -0.5 * pre_act * pre_act
    )


def layer_norm(hidden):
    centred = hidden - jnp.mean(hidden, axis=-1, keepdims=True)
    inverse = lax.rsqrt(jnp.mean(centred * centred, axis=-1, keepdims=True) + EPSILON)
    return (centred * inverse, inverse)


def norm_backward(upstream, normed, inverse, gain):
    scaled = upstream * gain
    return inverse * (
        scaled
        - jnp.mean(scaled, axis=-1, keepdims=True)
        - normed * jnp.mean(scaled * normed, axis=-1, keepdims=True)
    )


def contract_rows(former, latter):
    return lax.dot_general(
        former, latter, (((0,), (0,)), ((), ())), preferred_element_type=jnp.float32
    )


def times_transposed(former, latter):
    return lax.dot_general(
        former, latter, (((1,), (1,)), ((), ())), preferred_element_type=jnp.float32
    )


def split_heads(matrix):
    return matrix.reshape(matrix.shape[0] // LEN, LEN, HEADS, HEAD_DIM)


def merge_heads(tensor):
    return tensor.reshape(tensor.shape[0] * LEN, HEADS * HEAD_DIM)


def score_block(query_rows, key_rows, lengths):
    scores = jnp.einsum(
        "sqhd,skhd->shqk",
        split_heads(query_rows),
        split_heads(key_rows),
        preferred_element_type=jnp.float32,
    ) * HEAD_DIM ** (-0.5)
    positions = jnp.arange(LEN, dtype=jnp.int32)
    usable = (positions[None, :] < lengths[:, None])[:, None, None, :]
    return (scores, usable)


def attention_backward(query_rows, key_rows, value_rows, log_total, lengths, grad_context):
    scores, usable = score_block(query_rows, key_rows, lengths)
    exact = jnp.where(usable, jnp.exp(scores - log_total), 0.0)
    shares = exact.astype(jnp.bfloat16)
    context_heads = split_heads(grad_context)
    grad_value = jnp.einsum(
        "shqk,sqhd->skhd", shares, context_heads, preferred_element_type=jnp.float32
    )
    grad_shares = jnp.einsum(
        "sqhd,skhd->shqk",
        context_heads,
        split_heads(value_rows),
        preferred_element_type=jnp.float32,
    )
    grad_scores = (
        exact
        * (grad_shares - jnp.sum(exact * grad_shares, axis=-1, keepdims=True))
        * HEAD_DIM ** (-0.5)
    ).astype(jnp.bfloat16)
    grad_query = jnp.einsum(
        "shqk,skhd->sqhd", grad_scores, split_heads(key_rows), preferred_element_type=jnp.float32
    )
    grad_key = jnp.einsum(
        "shqk,sqhd->skhd", grad_scores, split_heads(query_rows), preferred_element_type=jnp.float32
    )
    return (merge_heads(grad_query), merge_heads(grad_key), merge_heads(grad_value))


def per_device(
    tokens,
    lengths,
    qkv_weight,
    query_bias,
    value_bias,
    proj_weight,
    proj_bias,
    attn_gain,
    attn_shift,
    up_weight,
    up_bias,
    down_weight,
    down_bias,
    ffn_gain,
    ffn_shift,
    cotangent,
):
    qkv_full, query_full, value_full, proj_full, proj_bias_full, attn_gain_full, attn_shift_full = (
        lax.all_gather(qkv_weight, "shard", axis=0, tiled=True),
        lax.all_gather(query_bias, "shard", axis=0, tiled=True),
        lax.all_gather(value_bias, "shard", axis=0, tiled=True),
        lax.all_gather(proj_weight, "shard", axis=0, tiled=True),
        lax.all_gather(proj_bias, "shard", axis=0, tiled=True),
        lax.all_gather(attn_gain, "shard", axis=0, tiled=True),
        lax.all_gather(attn_shift, "shard", axis=0, tiled=True),
    )
    model_width = tokens.shape[1]
    project = jnp.dot(tokens, qkv_full, preferred_element_type=jnp.float32)
    query_rows = (project[:, :model_width] + query_full.astype(jnp.float32)).astype(jnp.bfloat16)
    key_rows = project[:, model_width : 2 * model_width].astype(jnp.bfloat16)
    value_rows = (project[:, 2 * model_width :] + value_full.astype(jnp.float32)).astype(
        jnp.bfloat16
    )
    scores, usable = score_block(query_rows, key_rows, lengths)
    log_total = jnp.log(jnp.sum(jnp.where(usable, jnp.exp(scores), 0.0), axis=-1, keepdims=True))
    shares = jnp.where(usable, jnp.exp(scores - log_total), 0.0).astype(jnp.bfloat16)
    context = merge_heads(
        jnp.einsum(
            "shqk,skhd->sqhd", shares, split_heads(value_rows), preferred_element_type=jnp.float32
        )
    ).astype(jnp.bfloat16)
    attn_sum = (
        tokens.astype(jnp.float32)
        + jnp.dot(context, proj_full, preferred_element_type=jnp.float32)
        + proj_bias_full.astype(jnp.float32)
    )
    normed_one, inverse_one = layer_norm(attn_sum)
    mid_state = normed_one * attn_gain_full.astype(jnp.float32) + attn_shift_full.astype(
        jnp.float32
    )
    mid_half = mid_state.astype(jnp.bfloat16)
    up_full, up_bias_full, down_full, down_bias_full, ffn_gain_full, ffn_shift_full = (
        lax.all_gather(up_weight, "shard", axis=0, tiled=True),
        lax.all_gather(up_bias, "shard", axis=0, tiled=True),
        lax.all_gather(down_weight, "shard", axis=0, tiled=True),
        lax.all_gather(down_bias, "shard", axis=0, tiled=True),
        lax.all_gather(ffn_gain, "shard", axis=0, tiled=True),
        lax.all_gather(ffn_shift, "shard", axis=0, tiled=True),
    )
    pre_act = jnp.dot(mid_half, up_full, preferred_element_type=jnp.float32) + up_bias_full.astype(
        jnp.float32
    )
    hidden = gelu_value(pre_act).astype(jnp.bfloat16)
    ffn_sum = (
        mid_state
        + jnp.dot(hidden, down_full, preferred_element_type=jnp.float32)
        + down_bias_full.astype(jnp.float32)
    )
    normed_two, inverse_two = layer_norm(ffn_sum)
    layer_output = (
        normed_two * ffn_gain_full.astype(jnp.float32) + ffn_shift_full.astype(jnp.float32)
    ).astype(jnp.bfloat16)
    token_cols, context_cols, mid_cols, hidden_cols = (
        lax.all_to_all(tokens, "shard", split_axis=1, concat_axis=0, tiled=True),
        lax.all_to_all(context, "shard", split_axis=1, concat_axis=0, tiled=True),
        lax.all_to_all(mid_half, "shard", split_axis=1, concat_axis=0, tiled=True),
        lax.all_to_all(hidden, "shard", split_axis=1, concat_axis=0, tiled=True),
    )
    upstream = cotangent.astype(jnp.float32)
    grad_ffn_shift = jnp.sum(upstream, axis=0)
    grad_ffn_gain = jnp.sum(upstream * normed_two, axis=0)
    grad_ffn_sum = norm_backward(
        upstream, normed_two, inverse_two, ffn_gain_full.astype(jnp.float32)
    )
    ffn_half = grad_ffn_sum.astype(jnp.bfloat16)
    grad_down_bias = jnp.sum(grad_ffn_sum, axis=0)
    grad_pre = times_transposed(ffn_half, down_full) * gelu_slope(pre_act)
    pre_half = grad_pre.astype(jnp.bfloat16)
    grad_up_bias = jnp.sum(grad_pre, axis=0)
    grad_mid = grad_ffn_sum + times_transposed(pre_half, up_full)
    pre_group, ffn_group = (
        lax.all_gather(pre_half, "shard", axis=0, tiled=True),
        lax.all_gather(ffn_half, "shard", axis=0, tiled=True),
    )
    ffn_vecs = (
        lax.psum_scatter(grad_up_bias, "shard", scatter_dimension=0, tiled=True),
        lax.psum_scatter(grad_down_bias, "shard", scatter_dimension=0, tiled=True),
        lax.psum_scatter(grad_ffn_gain, "shard", scatter_dimension=0, tiled=True),
        lax.psum_scatter(grad_ffn_shift, "shard", scatter_dimension=0, tiled=True),
    )
    ffn_shares = (
        contract_rows(mid_cols, pre_group),
        ffn_vecs[0],
        contract_rows(hidden_cols, ffn_group),
        ffn_vecs[1],
        ffn_vecs[2],
        ffn_vecs[3],
    )
    grad_attn_shift = jnp.sum(grad_mid, axis=0)
    grad_attn_gain = jnp.sum(grad_mid * normed_one, axis=0)
    grad_attn_sum = norm_backward(
        grad_mid, normed_one, inverse_one, attn_gain_full.astype(jnp.float32)
    )
    attn_half = grad_attn_sum.astype(jnp.bfloat16)
    grad_proj_bias = jnp.sum(grad_attn_sum, axis=0)
    grad_context = times_transposed(attn_half, proj_full).astype(jnp.bfloat16)
    grad_query, grad_key, grad_value = attention_backward(
        query_rows, key_rows, value_rows, log_total, lengths, grad_context
    )
    grad_query_bias = jnp.sum(grad_query, axis=0)
    grad_value_bias = jnp.sum(grad_value, axis=0)
    grad_packed = jnp.concatenate([grad_query, grad_key, grad_value], axis=1).astype(jnp.bfloat16)
    grad_tokens = (grad_attn_sum + times_transposed(grad_packed, qkv_full)).astype(jnp.bfloat16)
    packed_group, attn_group = (
        lax.all_gather(grad_packed, "shard", axis=0, tiled=True),
        lax.all_gather(attn_half, "shard", axis=0, tiled=True),
    )
    attn_vecs = (
        lax.psum_scatter(grad_query_bias, "shard", scatter_dimension=0, tiled=True),
        lax.psum_scatter(grad_value_bias, "shard", scatter_dimension=0, tiled=True),
        lax.psum_scatter(grad_proj_bias, "shard", scatter_dimension=0, tiled=True),
        lax.psum_scatter(grad_attn_gain, "shard", scatter_dimension=0, tiled=True),
        lax.psum_scatter(grad_attn_shift, "shard", scatter_dimension=0, tiled=True),
    )
    attn_shares = (
        contract_rows(token_cols, packed_group),
        attn_vecs[0],
        attn_vecs[1],
        contract_rows(context_cols, attn_group),
        attn_vecs[2],
        attn_vecs[3],
        attn_vecs[4],
    )
    summed = (
        lax.psum(attn_shares[0].astype(jnp.bfloat16), "rep").astype(jnp.float32),
        lax.psum(attn_shares[1].astype(jnp.bfloat16), "rep").astype(jnp.float32),
        lax.psum(attn_shares[2].astype(jnp.bfloat16), "rep").astype(jnp.float32),
        lax.psum(attn_shares[3].astype(jnp.bfloat16), "rep").astype(jnp.float32),
        lax.psum(attn_shares[4].astype(jnp.bfloat16), "rep").astype(jnp.float32),
        lax.psum(attn_shares[5].astype(jnp.bfloat16), "rep").astype(jnp.float32),
        lax.psum(attn_shares[6].astype(jnp.bfloat16), "rep").astype(jnp.float32),
        lax.psum(ffn_shares[0].astype(jnp.bfloat16), "rep").astype(jnp.float32),
        lax.psum(ffn_shares[1].astype(jnp.bfloat16), "rep").astype(jnp.float32),
        lax.psum(ffn_shares[2].astype(jnp.bfloat16), "rep").astype(jnp.float32),
        lax.psum(ffn_shares[3].astype(jnp.bfloat16), "rep").astype(jnp.float32),
        lax.psum(ffn_shares[4].astype(jnp.bfloat16), "rep").astype(jnp.float32),
        lax.psum(ffn_shares[5].astype(jnp.bfloat16), "rep").astype(jnp.float32),
    )
    return (
        layer_output,
        grad_tokens,
        summed[0],
        summed[1],
        summed[2],
        summed[3],
        summed[4],
        summed[5],
        summed[6],
        summed[7],
        summed[8],
        summed[9],
        summed[10],
        summed[11],
        summed[12],
    )


def solution(mesh):
    placed = (
        P(("rep", "shard"), None),
        P(("rep", "shard")),
        P("shard", None),
        P("shard"),
        P("shard"),
        P("shard", None),
        P("shard"),
        P("shard"),
        P("shard"),
        P("shard", None),
        P("shard"),
        P("shard", None),
        P("shard"),
        P("shard"),
        P("shard"),
        P(("rep", "shard"), None),
    )
    return jax.shard_map(
        per_device,
        mesh=mesh,
        in_specs=placed,
        out_specs=(
            P(("rep", "shard"), None),
            P(("rep", "shard"), None),
            P("shard", None),
            P("shard"),
            P("shard"),
            P("shard", None),
            P("shard"),
            P("shard"),
            P("shard"),
            P("shard", None),
            P("shard"),
            P("shard", None),
            P("shard"),
            P("shard"),
            P("shard"),
        ),
        check_vma=False,
    )
```

profile of v0, /device:TPU:0, one launch (start us, length us, event | category | flops | bytes accessed | tf_op | source)
XLA Modules:
  0.0 712.5 jit_solution(2446243803208572598)
XLA Ops:
  7.2 0.7 all-gather.15.cloned.1.call-update
  8.0 0.7 all-gather.17.cloned.1.call-update
  8.7 0.7 all-gather.19.cloned.1.call-update
  10.1 5.3 all-gather.5
  15.5 4.4 all_gather.59
  19.9 4.4 all-gather.2
  24.2 4.6 all-gather.1
  28.8 4.5 all-gather
  34.1 4.5 all-gather.4
  38.6 4.5 all-gather.3
  43.2 4.5 all-gather.6
  47.8 4.5 all-gather.7
  52.3 40.6 %all-gather.15.cloned.1.call-done = bf16[1024,3072]{1,0:T(8,128)(2,1)} async-done(((bf16[512,3072]{1,0:T(8,128)(2,1)}), bf16[1024,3072]{1,0:T(8,128)(2,1)}) %all-gather.15.cloned.1.call-update) | async-done | bytes 6291472 | tf_op jit(solution)/shard_map/all_gather | solution.py:118
  92.9 3.8 fusion.58
  98.2 29.3 %all-gather.17.cloned.1.call-done = bf16[1024,1024]{1,0:T(8,128)(2,1)} async-done(((bf16[512,1024]{1,0:T(8,128)(2,1)}), bf16[1024,1024]{1,0:T(8,128)(2,1)}) %all-gather.17.cloned.1.call-update) | async-done | bytes 2097168 | tf_op jit(solution)/shard_map/all_gather | solution.py:121
  127.6 2.1 fusion.54
  130.2 1.3 fusion.12
  131.5 101.7 %all-gather.19.cloned.1.call-done = bf16[1024,4096]{1,0:T(8,128)(2,1)} async-done(((bf16[512,4096]{1,0:T(8,128)(2,1)}), bf16[1024,4096]{1,0:T(8,128)(2,1)}) %all-gather.19.cloned.1.call-update) | async-done | bytes 8388624 | tf_op jit(solution)/shard_map/all_gather | solution.py:152
  233.1 6.3 multiply_convert_fusion
  239.5 99.1 %all-gather.21.cloned.1.call-done = bf16[4096,1024]{1,0:T(8,128)(2,1)} async-done(((bf16[2048,1024]{1,0:T(8,128)(2,1)}), bf16[4096,1024]{1,0:T(8,128)(2,1)}) %all-gather.21.cloned.1.call-update) | async-done | bytes 8388624 | tf_op jit(solution)/shard_map/all_gather | solution.py:154
  338.6 4.9 fusion.55
  344.0 1.0 fusion.48
  345.3 3.3 fusion.51
  348.6 6.8 multiply_reduce_fusion.1
  355.7 1.3 copy-done
  357.0 0.8 convolution_convert_fusion.5
  358.1 0.7 copy-done.16
  358.8 3.0 fusion.52
  361.7 1.4 fusion.59
  363.1 2.8 convolution_convert_fusion.4
  366.0 2.7 fusion.53
  368.6 2.1 pad_maximum_fusion
  371.3 0.8 copy.78
  372.2 3.4 all-to-all-start
  375.6 0.9 copy.80
  376.5 4.4 all-to-all-done
  380.9 3.4 all-to-all-start.1
  384.5 0.7 copy.93
  385.2 1.0 copy.92
  386.2 6.8 all-to-all-done.1
  393.0 3.6 all-to-all-start.3
  396.6 23.8 %all_gather.65 = bf16[256,1024]{1,0:T(8,128)(2,1)S(1)} all-gather(bf16[128,1024]{1,0:T(8,128)(2,1)S(1)} %convert_element_type.198), channel_id=1, replica_groups=mesh['rep'=16,'shard'=2] {'shard'}, dimensions={0}, use_global_device_ids=true | all-gather | bytes 786432 | tf_op jit(solution)/shard_map/all_gather | solution.py:225
  420.4 14.4 %all_gather.67 = bf16[256,1024]{1,0:T(8,128)(2,1)S(1)} all-gather(bf16[128,1024]{1,0:T(8,128)(2,1)S(1)} %copy-done.10), channel_id=1, replica_groups=mesh['rep'=16,'shard'=2] {'shard'}, dimensions={0}, use_global_device_ids=true | all-gather | bytes 786432 | tf_op jit(solution)/shard_map/all_gather | solution.py:192
  434.8 1.4 convolution_convert_fusion.3
  436.2 3.4 all-to-all-start.2
  439.7 3.3 convolution_convert_fusion.2
  443.0 4.1 fusion.2
  447.1 0.7 all-to-all-done.2
  447.8 0.9 all-gather.25.cloned.1.call-done
  448.6 4.9 convolution_convert_fusion
  453.6 0.6 copy-done.31
  454.2 0.6 dynamic-slice
  456.2 7.5 %all-reduce.9 = (bf16[1024]{0:T(1024)(128)(2,1)S(1)}, bf16[1024]{0:T(1024)(128)(2,1)S(1)}, bf16[1024]{0:T(1024)(128)(2,1)S(1)}, bf16[1024]{0:T(1024)(128)(2,1)S(...) all-reduce(f32[1024]{0:T(1024)S(1)} %reduce_sum.186, ...), channel_id=2, replica_groups=mesh['rep'=16,'shard'=2] {'shard'}, use_global_device_ids=true, to_apply=%region_12.13.clone | all-reduce | flops 12288 | bytes 73728
  464.3 63.1 %all-reduce.10 = (bf16[512]{0:T(512)(128)(2,1)S(1)}, bf16[512]{0:T(512)(128)(2,1)S(1)}, bf16[512]{0:T(512)(128)(2,1)S(1)}, bf16[512]{0:T(512)(128)(2,1)S(1)}, bf...) all-reduce(bf16[512]{0:T(512)(128)(2,1)S(1)} %dynamic-slice.35, ...), channel_id=1, replica_groups=mesh['rep'=16,'shard'=2] {'rep'}, use_global_device_ids=true, to_apply=%region_13.14 | all-reduce | flops 6144 | bytes 24576 | tf_op jit(solution)/shard_map/psum | solution.py:245
  530.3 0.6 convert_element_type.221
  530.9 0.6 convert_element_type.225
  531.4 0.6 convert_element_type.227
  532.0 0.6 convert_element_type.229
  532.6 5.8 fusion.16
  538.4 148.9 %all-reduce.14.cloned.1.call-done = (bf16[512,3072]{0,1:T(8,128)(2,1)}, bf16[512,1024]{1,0:T(8,128)(2,1)}, bf16[512,4096]{1,0:T(8,128)(2,1)}, bf16[2048,1024]{1,0:T(8,128)(2,1)}) async-done(((bf16[512,3072]{0,1:T(8,128)(2,1)}, bf16[512,1024]{1,0:T(8,128)(2,1)}, bf16[512,4096]{1,0:T(8,128)(2,1)}, bf16[2048,1024]{1,0:T(8,128)(2,1)}), (bf16[512,3072]{0,1:T(8,128)(2,1)}, bf16[512,1024]{1,0:T(8,128)(2,1)}, ...) | async-done | bytes 12582928 | tf_op jit(solution)/shard_map/psum | solution.py:244
  687.3 5.5 copy.83
  692.8 1.6 convert_element_type.211
  694.4 6.8 convert_element_type.219
  701.2 4.4 convert_element_type.223
  (136 shorter events, 8.4 us)
Async XLA Ops:
  7.2 85.7 %all-gather.15.cloned.1.call-start = ((), (), s32[]{:S(2)}) async-start(), calls=%async_computation.4 | async-start | bytes 9437184 | tf_op jit(solution)/shard_map/all_gather | solution.py:118
  7.9 119.7 %all-gather.17.cloned.1.call-start = ((), (), s32[]{:S(2)}) async-start(), calls=%async_computation.5 | async-start | bytes 3145728 | tf_op jit(solution)/shard_map/all_gather | solution.py:121
  8.7 224.5 %all-gather.19.cloned.1.call-start = ((), (), s32[]{:S(2)}) async-start(), calls=%async_computation.6 | async-start | bytes 12582912 | tf_op jit(solution)/shard_map/all_gather | solution.py:152
  9.4 0.7 copy-start.23
  9.4 6.1 copy-start.22
  9.4 10.4 %copy-start.24 = (bf16[512]{0:T(512)(128)(2,1)S(1)}, bf16[512]{0:T(512)(128)(2,1)}, u32[]{:S(2)}) copy-start(bf16[512]{0:T(512)(128)(2,1)} %param.22) | copy-start | bytes 3076
  9.4 14.8 %copy-start.25 = (bf16[512]{0:T(512)(128)(2,1)S(1)}, bf16[512]{0:T(512)(128)(2,1)}, u32[]{:S(2)}) copy-start(bf16[512]{0:T(512)(128)(2,1)} %param.19) | copy-start | bytes 3076
  9.4 19.4 %copy-start.26 = (bf16[512]{0:T(512)(128)(2,1)S(1)}, bf16[512]{0:T(512)(128)(2,1)}, u32[]{:S(2)}) copy-start(bf16[512]{0:T(512)(128)(2,1)} %param.20) | copy-start | bytes 3076
  9.5 24.6 %copy-start.27 = (bf16[512]{0:T(512)(128)(2,1)S(1)}, bf16[512]{0:T(512)(128)(2,1)}, u32[]{:S(2)}) copy-start(bf16[512]{0:T(512)(128)(2,1)} %param.24) | copy-start | bytes 3076
  9.5 29.1 %copy-start.28 = (bf16[512]{0:T(512)(128)(2,1)S(1)}, bf16[512]{0:T(512)(128)(2,1)}, u32[]{:S(2)}) copy-start(bf16[512]{0:T(512)(128)(2,1)} %param.23) | copy-start | bytes 3076
  9.5 33.7 %copy-start.29 = (bf16[512]{0:T(512)(128)(2,1)S(1)}, bf16[512]{0:T(512)(128)(2,1)}, u32[]{:S(2)}) copy-start(bf16[512]{0:T(512)(128)(2,1)} %param.29) | copy-start | bytes 3076
  9.5 38.3 %copy-start.30 = (bf16[512]{0:T(512)(128)(2,1)S(1)}, bf16[512]{0:T(512)(128)(2,1)}, u32[]{:S(2)}) copy-start(bf16[512]{0:T(512)(128)(2,1)} %param.30) | copy-start | bytes 3076
  9.5 83.4 %copy-start.3 = (bf16[128,1024]{1,0:T(8,128)(2,1)S(1)}, bf16[128,1024]{1,0:T(8,128)(2,1)}, u32[]{:S(2)}) copy-start(bf16[128,1024]{1,0:T(8,128)(2,1)} %param.16) | copy-start | bytes 786436
  9.5 329.1 %all-gather.21.cloned.1.call-start = ((), (), s32[]{:S(2)}) async-start(), calls=%async_computation.7 | async-start | bytes 12582912 | tf_op jit(solution)/shard_map/all_gather | solution.py:154
  10.1 433.0 %all-gather.23.cloned.1.call-start = ((), (), s32[]{:S(2)}) async-start(), calls=%async_computation.8 | async-start | bytes 2359296 | tf_op jit(solution)/shard_map/all_gather | solution.py:224
  97.0 1.2 copy-start.14
  97.2 30.4 %copy-start.15 = (bf16[128,1024]{0,1:T(8,128)(2,1)}, bf16[128,1024]{0,1:T(8,128)(2,1)S(1)}, u32[]{:S(2)}) copy-start(bf16[128,1024]{0,1:T(8,128)(2,1)S(1)} %copy.71) | copy-start | bytes 786436
  97.4 32.4 %copy-start.12 = (bf16[128,1024]{0,1:T(8,128)(2,1)}, bf16[128,1024]{0,1:T(8,128)(2,1)S(1)}, u32[]{:S(2)}) copy-start(bf16[128,1024]{0,1:T(8,128)(2,1)S(1)} %copy.72) | copy-start | bytes 786436
  97.7 32.4 %copy-start.11 = (f32[16,128,128]{1,2,0:T(8,128)}, f32[16,128,128]{1,2,0:T(8,128)S(1)}, u32[]{:S(2)}) copy-start(f32[16,128,128]{1,2,0:T(8,128)S(1)} %convolution_multiply_fusion.1) | copy-start | bytes 3145732
  98.2 31.7 %copy-start.17 = (bf16[16,64,128]{2,1,0:T(8,128)(2,1)}, bf16[16,64,128]{2,1,0:T(8,128)(2,1)S(1)}, u32[]{:S(2)}) copy-start(bf16[16,64,128]{2,1,0:T(8,128)(2,1)S(1)} %convolution_convert_fusion.6) | copy-start | bytes 786436
  130.1 109.3 %copy-start.4 = (bf16[128,1024]{1,0:T(8,128)(2,1)}, bf16[128,1024]{1,0:T(8,128)(2,1)S(1)}, u32[]{:S(2)}) copy-start(bf16[128,1024]{1,0:T(8,128)(2,1)S(1)} %fusion.36) | copy-start | bytes 786436
  338.6 6.5 slice-start
  338.6 5.2 copy-start.8
  338.6 6.5 slice-start.1
  343.5 1.8 copy-start.6
  345.0 3.6 copy-start.9
  348.6 6.8 copy-start.2
  355.5 1.6 copy-start
  358.1 0.7 copy-start.16
  358.8 7.2 %copy-start.13 = (bf16[128,1024]{0,1:T(8,128)(2,1)S(1)}, bf16[128,1024]{0,1:T(8,128)(2,1)}, u32[]{:S(2)}) copy-start(bf16[128,1024]{0,1:T(8,128)(2,1)} %copy-done.12) | copy-start | bytes 786436
  368.6 7.0 copy-start.18
  370.7 13.8 %copy-start.5 = (bf16[128,1024]{1,0:T(8,128)(2,1)S(1)}, bf16[128,1024]{1,0:T(8,128)(2,1)}, u32[]{:S(2)}) copy-start(bf16[128,1024]{1,0:T(8,128)(2,1)} %copy-done.4) | copy-start | bytes 786436
  370.7 77.9 %all-gather.25.cloned.1.call-start = ((), (), s32[]{:S(2)}) async-start(), calls=%async_computation.9 | async-start | bytes 3145728 | tf_op jit(solution)/shard_map/all_gather | solution.py:191
  372.2 8.7 %all-to-all-start = ((bf16[128,2,512]{0,2,1:T(8,128)(2,1)}), bf16[128,2,512]{0,2,1:T(8,128)(2,1)S(1)}, u32[]{:S(2)}, u32[]{:S(2)}) async-start(bf16[128,2,512]{0,2,1:T(8,128)(2,1)} %bitcast.25), calls=%async_computation | async-start | bytes 524288 | tf_op jit(solution)/shard_map/all_to_all | solution.py:173
  380.9 12.1 %all-to-all-start.1 = ((bf16[128,2,512]{2,0,1:T(8,128)(2,1)}), bf16[128,2,512]{2,0,1:T(8,128)(2,1)S(1)}, u32[]{:S(2)}, u32[]{:S(2)}) async-start(bf16[128,2,512]{2,0,1:T(8,128)(2,1)} %copy.80), calls=%async_computation.1 | async-start | bytes 524288 | tf_op jit(solution)/shard_map/all_to_all | solution.py:174
  385.2 35.2 %copy-start.10 = (bf16[128,1024]{1,0:T(8,128)(2,1)S(1)}, bf16[128,1024]{1,0:T(8,128)(2,1)}, u32[]{:S(2)}) copy-start(bf16[128,1024]{1,0:T(8,128)(2,1)} %copy-done.9) | copy-start | bytes 786436
  393.0 43.2 %all-to-all-start.3 = ((bf16[128,2,2048]{2,0,1:T(8,128)(2,1)}), bf16[128,2,2048]{2,0,1:T(8,128)(2,1)S(1)}, u32[]{:S(2)}, u32[]{:S(2)}) async-start(bf16[128,2,2048]{2,0,1:T(8,128)(2,1)} %bitcast.87), calls=%async_computation.3 | async-start | bytes 2097152 | tf_op jit(solution)/shard_map/all_to_all | solution.py:176
  436.2 11.5 %all-to-all-start.2 = ((bf16[128,2,512]{2,0,1:T(8,128)(2,1)}), bf16[128,2,512]{2,0,1:T(8,128)(2,1)S(1)}, u32[]{:S(2)}, u32[]{:S(2)}) async-start(bf16[128,2,512]{2,0,1:T(8,128)(2,1)} %bitcast.88), calls=%async_computation.2 | async-start | bytes 524288 | tf_op jit(solution)/shard_map/all_to_all | solution.py:175
  439.7 247.7 %all-reduce.14.cloned.1.call-start = ((), (), s32[]{:S(2)}) async-start(), calls=%async_computation.10 | async-start | bytes 25165824 | tf_op jit(solution)/shard_map/psum | solution.py:244
  453.5 0.7 copy-start.31
  453.5 79.1 %copy-start.19 = (bf16[1,128,16,64]{1,3,2,0:T(8,128)(2,1)S(1)}, bf16[1,128,16,64]{1,3,2,0:T(8,128)(2,1)}, u32[]{:S(2)}) copy-start(bf16[1,128,16,64]{1,3,2,0:T(8,128)(2,1)} %get-tuple-element.115) | copy-start | bytes 786436
  453.5 79.1 %copy-start.20 = (bf16[16,64,128]{2,1,0:T(8,128)(2,1)S(1)}, bf16[16,64,128]{2,1,0:T(8,128)(2,1)}, u32[]{:S(2)}) copy-start(bf16[16,64,128]{2,1,0:T(8,128)(2,1)} %convolution_convert_fusion.4) | copy-start | bytes 786436
  453.5 79.1 %copy-start.21 = (bf16[1,128,16,64]{1,3,2,0:T(8,128)(2,1)S(1)}, bf16[1,128,16,64]{1,3,2,0:T(8,128)(2,1)}, u32[]{:S(2)}) copy-start(bf16[1,128,16,64]{1,3,2,0:T(8,128)(2,1)} %get-tuple-element.117) | copy-start | bytes 786436
  687.3 5.5 copy-start.7
  694.4 6.8 copy-start.1
Sparse Core Ops, SparseCore 0:
  9.5 83.3 all-gather.14
  94.4 33.1 all-gather.16
  129.1 103.9 all-gather.18
  234.5 103.9 all-gather.20
  370.9 32.3 all-gather.22
  404.6 43.9 all-gather.24
  454.3 232.9 all-reduce.13
where the time goes:
time: 714 us; the launch traced here: 712 us
  waiting for transfers between devices  435 us (61%)
  blocking collectives  150 us (21%)
  matrix products  58.3 us (8%)
  other arithmetic  23.7 us (3%)
  between operations  16.7 us (2%)
  starting transfers between devices  14.2 us (2%)
  local copies, waits for them, and re-layouts  14.2 us (2%)
    psum x1, waiting for transfers between devices, per_device(): lax.psum(attn_shares[0].astype(jnp.bfloat16), 'rep').astype(jnp.float32)  149 us
    all_gather x1, waiting for transfers between devices, per_device(): lax.all_gather(up_weight, 'shard', axis=0, tiled=True)  102 us
    all_gather x1, waiting for transfers between devices, per_device(): lax.all_gather(down_weight, 'shard', axis=0, tiled=True)  99.1 us
    psum x1, blocking collectives, per_device(): lax.psum(attn_shares[1].astype(jnp.bfloat16), 'rep').astype(jnp.float32)  63.1 us
    all_gather x1, waiting for transfers between devices, per_device(): lax.all_gather(qkv_weight, 'shard', axis=0, tiled=True)  40.6 us
    all_gather x1, waiting for transfers between devices, per_device(): lax.all_gather(proj_weight, 'shard', axis=0, tiled=True)  29.3 us
    all_gather x1, blocking collectives, per_device(): lax.all_gather(attn_half, 'shard', axis=0, tiled=True)  23.8 us
    dot_general x4, matrix products, times_transposed(): lax.dot_general(former, latter, (((1,), (1,)), ((), ())), preferred_eleme...  16.7 us
  transfers between devices with their start and end apart: 11, of which 9 were waited for; matrix products, arithmetic and copies ran while one was open for 6% of the time, Pallas kernels for 0%

commit v1 on v0

--- a/solution.py
+++ b/solution.py
@@ -9,6 +9,18 @@
 EPSILON = 1e-05
 SQRT_HALF = 0.7071067811865476
 INV_ROOT_TAU = 0.3989422804014327
+
+
+def gather_by_bits(value, axis, dim):
+    ways, here, step = (lax.axis_size(axis), lax.axis_index(axis), value.shape[dim])
+    line, have = (value, 1)
+    while have < ways:
+        line = jnp.concatenate(
+            [line, lax.ppermute(line, axis, [(d, (d - have) % ways) for d in range(ways)])],
+            axis=dim,
+        )
+        have = 2 * have
+    return jnp.roll(line, here * step, axis=dim)
 
 
 def gelu_value(pre_act):
@@ -149,7 +161,7 @@
     )
     mid_half = mid_state.astype(jnp.bfloat16)
     up_full, up_bias_full, down_full, down_bias_full, ffn_gain_full, ffn_shift_full = (
-        lax.all_gather(up_weight, "shard", axis=0, tiled=True),
+        gather_by_bits(up_weight, "shard", 0),
         lax.all_gather(up_bias, "shard", axis=0, tiled=True),
         lax.all_gather(down_weight, "shard", axis=0, tiled=True),
         lax.all_gather(down_bias, "shard", axis=0, tiled=True),

time: 714 us -> 676 us (0.947)
  waiting for transfers between devices: 435 us -> 228 us
  blocking collectives: 150 us -> 303 us
  other arithmetic: 23.7 us -> 37.5 us
    all_gather x1, blocking collectives: 5.32 us -> 158 us  [per_device(): lax.all_gather(down_bias, 'shard', axis=0, tiled=True)]
    all_gather x1 -> x0, waiting for transfers between devices: 102 us -> none  [per_device(): lax.all_gather(up_weight, 'shard', axis=0, tiled=True)]
    all_gather x1, waiting for transfers between devices: 40.6 us -> 0.01 us  [per_device(): lax.all_gather(qkv_weight, 'shard', axis=0, tiled=True)]
    all_gather x1, waiting for transfers between devices: 99.1 us -> 64.3 us  [per_device(): lax.all_gather(down_weight, 'shard', axis=0, tiled=True)]
    all_gather x1, waiting for transfers between devices: 29.3 us -> 0.02 us  [per_device(): lax.all_gather(proj_weight, 'shard', axis=0, tiled=True)]
    concatenate x0 -> x1, other arithmetic: none -> 13.8 us  [gather_by_bits(): return jnp.roll(line, here * step, axis=dim)]
  transfers between devices with their start and end apart: 11 -> 11, of which waited for: 9 -> 6; matrix products, arithmetic and copies ran while one was open for 6% -> 8% of each run, Pallas kernels for 0% -> 0%
where the time goes in v1:
time: 676 us; the launch traced here: 675 us
  blocking collectives  303 us (45%)
  waiting for transfers between devices  228 us (34%)
  matrix products  58.4 us (9%)
  other arithmetic  37.5 us (6%)
  starting transfers between devices  17.2 us (3%)
  between operations  16.7 us (2%)
  local copies, waits for them, and re-layouts  14.2 us (2%)
    all_gather x1, blocking collectives, per_device(): lax.all_gather(down_bias, 'shard', axis=0, tiled=True)  158 us
    psum x1, waiting for transfers between devices, per_device(): lax.psum(attn_shares[0].astype(jnp.bfloat16), 'rep').astype(jnp.float32)  149 us
    all_gather x1, waiting for transfers between devices, per_device(): lax.all_gather(down_weight, 'shard', axis=0, tiled=True)  64.3 us
    psum x1, blocking collectives, per_device(): lax.psum(attn_shares[1].astype(jnp.bfloat16), 'rep').astype(jnp.float32)  63 us
    all_gather x1, blocking collectives, per_device(): lax.all_gather(attn_half, 'shard', axis=0, tiled=True)  23.8 us
    dot_general x4, matrix products, times_transposed(): lax.dot_general(former, latter, (((1,), (1,)), ((), ())), preferred_eleme...  16.9 us
    all_gather x1, blocking collectives, per_device(): lax.all_gather(ffn_half, 'shard', axis=0, tiled=True)  14.4 us
    concatenate x1, other arithmetic, gather_by_bits(): return jnp.roll(line, here * step, axis=dim)  13.8 us
  transfers between devices with their start and end apart: 11, of which 6 were waited for; matrix products, arithmetic and copies ran while one was open for 8% of the time, Pallas kernels for 0%

profile of v1, /device:TPU:0, one launch (start us, length us, event | category | flops | bytes accessed | tf_op | source)
XLA Modules:
  0.0 674.5 jit_solution(16786547974147117627)
XLA Ops:
  7.2 0.7 all-gather.14.cloned.1.call-update
  8.0 0.7 all-gather.16.cloned.1.call-update
  8.8 3.1 collective-permute-start
  12.0 158.3 %all-gather.5 = bf16[2,1,512]{2,1,0:T(2,128)(2,1)S(1)} all-gather(bf16[1,1,512]{2,1,0:T(2,128)(2,1)S(1)} %reshape.213), channel_id=1, replica_groups=mesh['rep'=16,'shard'=2] {'shard'}, dimensions={0}, use_global_device_ids=true | all-gather | bytes 3072 | tf_op jit(solution)/shard_map/all_gather | solution.py:167
  170.2 4.6 all_gather.55
  174.8 4.5 all-gather.2
  179.4 4.6 all-gather.1
  184.0 4.4 all-gather
  189.1 4.5 all-gather.4
  193.6 4.4 all-gather.3
  198.0 4.4 all-gather.6
  202.4 4.4 all-gather.7
  206.8 13.8 %fusion.4 = bf16[1024,4096]{1,0:T(8,128)(2,1)} fusion(s32[]{:T(128)S(6)} %select_n.26, bf16[512,4096]{1,0:T(8,128)(2,1)} %param.25, bf16[512,4096]{1,0:T(8,128)(2,1)} %collective-permute-done), kind=kLoop, calls=%fused_computation.8 | loop fusion | flops 33554432 | bytes 16777220 | tf_op jit(solution)/shard_map/jit(_roll_dynamic)/concatenate | solution.py:23
  220.7 3.8 fusion.61
  226.1 2.2 fusion.57
  228.7 1.3 fusion.15
  230.0 6.3 multiply_convert_fusion
  236.3 64.3 %all-gather.18.cloned.1.call-done = bf16[4096,1024]{1,0:T(8,128)(2,1)} async-done(((bf16[2048,1024]{1,0:T(8,128)(2,1)}), bf16[4096,1024]{1,0:T(8,128)(2,1)}) %all-gather.18.cloned.1.call-update) | async-done | bytes 8388624 | tf_op jit(solution)/shard_map/all_gather | solution.py:166
  300.7 4.9 fusion.58
  306.1 1.0 fusion.51
  307.5 3.4 fusion.54
  310.9 6.8 %multiply_reduce_fusion.1 = (f32[1024]{0:T(1024)S(1)}, f32[128]{0:T(128)S(1)}, f32[128]{0:T(128)S(1)}, f32[1024]{0:T(1024)S(1)}, f32[128,1024]{1,0:T(8,128)S(1)}) fusion(f32[128,1024]{1,0:T(8,128)S(1)} %get-tuple-element.119, f32[128]{0:T(128)S(1)} %add_rsqrt_fusion.1, f32[128]{0:T(128)S(1)} %broadcast_multiply_fusion.5, f32[1024]{0:T(1024)S(1)} %bitcast.117, ...), kind=kOutput, calls=%fused_computation.64 | convolution fusion | flops 1075050240 | bytes 11024384 | tf_op jit(solution)/shard_map/dot_general | solution.py:58
  318.0 1.3 copy-done
  319.3 0.8 convolution_convert_fusion.5
  320.4 0.7 copy-done.16
  321.1 2.9 fusion.55
  324.0 1.4 fusion.62
  325.4 2.8 convolution_convert_fusion.4
  328.2 2.6 fusion.56
  330.8 2.1 pad_maximum_fusion
  333.5 0.8 copy.78
  334.4 3.4 all-to-all-start
  337.8 0.9 copy.80
  338.7 4.4 all-to-all-done
  343.1 3.4 all-to-all-start.1
  346.7 0.7 copy.93
  347.4 1.0 copy.92
  348.4 6.8 %all-to-all-done.1 = bf16[128,2,512]{2,0,1:T(8,128)(2,1)S(1)} async-done(((bf16[128,2,512]{2,0,1:T(8,128)(2,1)}), bf16[128,2,512]{2,0,1:T(8,128)(2,1)S(1)}, u32[]{:S(2)}, u32[]{:S(2)}) %all-to-all-start.1) | async-done | bytes 262176 | tf_op jit(solution)/shard_map/all_to_all | solution.py:186
  355.2 3.6 all-to-all-start.3
  358.8 23.8 %all_gather.61 = bf16[256,1024]{1,0:T(8,128)(2,1)S(1)} all-gather(bf16[128,1024]{1,0:T(8,128)(2,1)S(1)} %convert_element_type.198), channel_id=1, replica_groups=mesh['rep'=16,'shard'=2] {'shard'}, dimensions={0}, use_global_device_ids=true | all-gather | bytes 786432 | tf_op jit(solution)/shard_map/all_gather | solution.py:237
  382.6 14.4 %all_gather.63 = bf16[256,1024]{1,0:T(8,128)(2,1)S(1)} all-gather(bf16[128,1024]{1,0:T(8,128)(2,1)S(1)} %copy-done.10), channel_id=1, replica_groups=mesh['rep'=16,'shard'=2] {'shard'}, dimensions={0}, use_global_device_ids=true | all-gather | bytes 786432 | tf_op jit(solution)/shard_map/all_gather | solution.py:204
  397.0 1.4 convolution_convert_fusion.3
  398.4 3.4 all-to-all-start.2
  401.9 3.3 convolution_convert_fusion.2
  405.2 4.0 fusion.5
  409.3 0.7 all-to-all-done.2
  410.0 0.9 all-gather.22.cloned.1.call-done
  410.8 4.9 convolution_convert_fusion
  415.8 0.6 copy-done.31
  416.4 0.6 dynamic-slice
  418.4 7.5 %all-reduce.9 = (bf16[1024]{0:T(1024)(128)(2,1)S(1)}, bf16[1024]{0:T(1024)(128)(2,1)S(1)}, bf16[1024]{0:T(1024)(128)(2,1)S(1)}, bf16[1024]{0:T(1024)(128)(2,1)S(...) all-reduce(f32[1024]{0:T(1024)S(1)} %reduce_sum.186, ...), channel_id=2, replica_groups=mesh['rep'=16,'shard'=2] {'shard'}, use_global_device_ids=true, to_apply=%region_12.13.clone | all-reduce | flops 12288 | bytes 73728
  426.5 63.0 %all-reduce.10 = (bf16[512]{0:T(512)(128)(2,1)S(1)}, bf16[512]{0:T(512)(128)(2,1)S(1)}, bf16[512]{0:T(512)(128)(2,1)S(1)}, bf16[512]{0:T(512)(128)(2,1)S(1)}, bf...) all-reduce(bf16[512]{0:T(512)(128)(2,1)S(1)} %dynamic-slice.35, ...), channel_id=1, replica_groups=mesh['rep'=16,'shard'=2] {'rep'}, use_global_device_ids=true, to_apply=%region_13.14 | all-reduce | flops 6144 | bytes 24576 | tf_op jit(solution)/shard_map/psum | solution.py:257
  489.6 0.6 convert_element_type.206
  490.1 0.6 convert_element_type.208
  490.7 0.6 convert_element_type.213
  491.3 0.6 convert_element_type.215
  491.9 0.6 convert_element_type.217
  492.5 0.6 convert_element_type.221
  494.8 5.8 fusion.19
  500.6 148.8 %all-reduce.14.cloned.1.call-done = (bf16[512,3072]{0,1:T(8,128)(2,1)}, bf16[512,1024]{1,0:T(8,128)(2,1)}, bf16[512,4096]{1,0:T(8,128)(2,1)}, bf16[2048,1024]{1,0:T(8,128)(2,1)}) async-done(((bf16[512,3072]{0,1:T(8,128)(2,1)}, bf16[512,1024]{1,0:T(8,128)(2,1)}, bf16[512,4096]{1,0:T(8,128)(2,1)}, bf16[2048,1024]{1,0:T(8,128)(2,1)}), (bf16[512,3072]{0,1:T(8,128)(2,1)}, bf16[512,1024]{1,0:T(8,128)(2,1)}, ...) | async-done | bytes 12582928 | tf_op jit(solution)/shard_map/psum | solution.py:256
  649.4 5.5 copy.83
  654.9 1.6 convert_element_type.211
  656.4 6.8 %convert_element_type.219 = f32[512,4096]{1,0:T(8,128)} convert(bf16[512,4096]{1,0:T(8,128)(2,1)} %get-tuple-element.103) | non-fusion elementwise | flops 2097152 | bytes 12582912 | tf_op jit(solution)/shard_map/convert_element_type | solution.py:263
  663.3 4.4 convert_element_type.223
  (136 shorter events, 6.8 us)
Async XLA Ops:
  7.2 213.5 %all-gather.14.cloned.1.call-start = ((), (), s32[]{:S(2)}) async-start(), calls=%async_computation.4 | async-start | bytes 9437184 | tf_op jit(solution)/shard_map/all_gather | solution.py:130
  7.9 218.1 %all-gather.16.cloned.1.call-start = ((), (), s32[]{:S(2)}) async-start(), calls=%async_computation.5 | async-start | bytes 3145728 | tf_op jit(solution)/shard_map/all_gather | solution.py:133
  8.7 3.3 copy-start.23
  8.7 161.5 %copy-start.22 = (bf16[2048]{0:T(1024)(128)(2,1)S(1)}, bf16[2048]{0:T(1024)(128)(2,1)}, u32[]{:S(2)}) copy-start(bf16[2048]{0:T(1024)(128)(2,1)} %param.26) | copy-start | bytes 12292
  8.7 166.1 %copy-start.24 = (bf16[512]{0:T(512)(128)(2,1)S(1)}, bf16[512]{0:T(512)(128)(2,1)}, u32[]{:S(2)}) copy-start(bf16[512]{0:T(512)(128)(2,1)} %param.22) | copy-start | bytes 3076
  8.7 170.7 %copy-start.25 = (bf16[512]{0:T(512)(128)(2,1)S(1)}, bf16[512]{0:T(512)(128)(2,1)}, u32[]{:S(2)}) copy-start(bf16[512]{0:T(512)(128)(2,1)} %param.19) | copy-start | bytes 3076
  8.7 175.2 %copy-start.26 = (bf16[512]{0:T(512)(128)(2,1)S(1)}, bf16[512]{0:T(512)(128)(2,1)}, u32[]{:S(2)}) copy-start(bf16[512]{0:T(512)(128)(2,1)} %param.20) | copy-start | bytes 3076
  8.7 180.3 %copy-start.27 = (bf16[512]{0:T(512)(128)(2,1)S(1)}, bf16[512]{0:T(512)(128)(2,1)}, u32[]{:S(2)}) copy-start(bf16[512]{0:T(512)(128)(2,1)} %param.24) | copy-start | bytes 3076
  8.7 184.9 %copy-start.28 = (bf16[512]{0:T(512)(128)(2,1)S(1)}, bf16[512]{0:T(512)(128)(2,1)}, u32[]{:S(2)}) copy-start(bf16[512]{0:T(512)(128)(2,1)} %param.23) | copy-start | bytes 3076
  8.7 189.3 %copy-start.29 = (bf16[512]{0:T(512)(128)(2,1)S(1)}, bf16[512]{0:T(512)(128)(2,1)}, u32[]{:S(2)}) copy-start(bf16[512]{0:T(512)(128)(2,1)} %param.29) | copy-start | bytes 3076
  8.7 193.7 %copy-start.30 = (bf16[512]{0:T(512)(128)(2,1)S(1)}, bf16[512]{0:T(512)(128)(2,1)}, u32[]{:S(2)}) copy-start(bf16[512]{0:T(512)(128)(2,1)} %param.30) | copy-start | bytes 3076
  8.8 291.9 %all-gather.18.cloned.1.call-start = ((), (), s32[]{:S(2)}) async-start(), calls=%async_computation.6 | async-start | bytes 12582912 | tf_op jit(solution)/shard_map/all_gather | solution.py:166
  8.8 198.0 %collective-permute-start = (bf16[512,4096]{1,0:T(8,128)(2,1)}, bf16[512,4096]{1,0:T(8,128)(2,1)}, u32[]{:S(2)}, u32[]{:S(2)}) collective-permute-start(bf16[512,4096]{1,0:T(8,128)(2,1)} %param.25), channel_id=1, source_target_pairs={{0,1},{1,0},{2,3},{3,2},{4,5},{5,4},{6,7},{7,6},{8,9},{9,8},{10,11... | collective-permute-start | bytes 12582920 | tf_op jit(solution)/shard_map/ppermute | solution.py:19
  11.9 393.4 %all-gather.20.cloned.1.call-start = ((), (), s32[]{:S(2)}) async-start(), calls=%async_computation.7 | async-start | bytes 2359296 | tf_op jit(solution)/shard_map/all_gather | solution.py:236
  206.8 13.9 %copy-start.3 = (bf16[128,1024]{1,0:T(8,128)(2,1)S(1)}, bf16[128,1024]{1,0:T(8,128)(2,1)}, u32[]{:S(2)}) copy-start(bf16[128,1024]{1,0:T(8,128)(2,1)} %param.16) | copy-start | bytes 786436
  224.8 1.2 copy-start.14
  225.0 3.3 copy-start.15
  225.1 0.9 copy-start.12
  225.5 3.2 copy-start.11
  226.0 2.7 copy-start.17
  228.7 7.6 %copy-start.4 = (bf16[128,1024]{1,0:T(8,128)(2,1)}, bf16[128,1024]{1,0:T(8,128)(2,1)S(1)}, u32[]{:S(2)}) copy-start(bf16[128,1024]{1,0:T(8,128)(2,1)S(1)} %fusion.39) | copy-start | bytes 786436
  300.7 6.5 slice-start
  300.7 5.2 copy-start.8
  300.7 6.5 slice-start.1
  305.6 1.8 copy-start.6
  307.1 3.8 copy-start.9
  310.9 6.8 %copy-start.2 = (bf16[128,4096]{1,0:T(8,128)(2,1)}, bf16[128,4096]{1,0:T(8,128)(2,1)S(1)}, u32[]{:S(2)}) copy-start(bf16[128,4096]{1,0:T(8,128)(2,1)S(1)} %get-tuple-element.110) | copy-start | bytes 3145732
  317.7 1.6 copy-start
  320.4 0.7 copy-start.16
  321.1 7.1 %copy-start.13 = (bf16[128,1024]{0,1:T(8,128)(2,1)S(1)}, bf16[128,1024]{0,1:T(8,128)(2,1)}, u32[]{:S(2)}) copy-start(bf16[128,1024]{0,1:T(8,128)(2,1)} %copy-done.12) | copy-start | bytes 786436
  330.8 7.0 %copy-start.18 = (bf16[16,64,128]{2,1,0:T(8,128)(2,1)S(1)}, bf16[16,64,128]{2,1,0:T(8,128)(2,1)}, u32[]{:S(2)}) copy-start(bf16[16,64,128]{2,1,0:T(8,128)(2,1)} %copy-done.17) | copy-start | bytes 786436
  332.9 13.8 %copy-start.5 = (bf16[128,1024]{1,0:T(8,128)(2,1)S(1)}, bf16[128,1024]{1,0:T(8,128)(2,1)}, u32[]{:S(2)}) copy-start(bf16[128,1024]{1,0:T(8,128)(2,1)} %copy-done.4) | copy-start | bytes 786436
  332.9 77.9 %all-gather.22.cloned.1.call-start = ((), (), s32[]{:S(2)}) async-start(), calls=%async_computation.8 | async-start | bytes 3145728 | tf_op jit(solution)/shard_map/all_gather | solution.py:203
  334.4 8.7 %all-to-all-start = ((bf16[128,2,512]{0,2,1:T(8,128)(2,1)}), bf16[128,2,512]{0,2,1:T(8,128)(2,1)S(1)}, u32[]{:S(2)}, u32[]{:S(2)}) async-start(bf16[128,2,512]{0,2,1:T(8,128)(2,1)} %bitcast.25), calls=%async_computation | async-start | bytes 524288 | tf_op jit(solution)/shard_map/all_to_all | solution.py:185
  343.1 12.1 %all-to-all-start.1 = ((bf16[128,2,512]{2,0,1:T(8,128)(2,1)}), bf16[128,2,512]{2,0,1:T(8,128)(2,1)S(1)}, u32[]{:S(2)}, u32[]{:S(2)}) async-start(bf16[128,2,512]{2,0,1:T(8,128)(2,1)} %copy.80), calls=%async_computation.1 | async-start | bytes 524288 | tf_op jit(solution)/shard_map/all_to_all | solution.py:186
  347.4 35.2 %copy-start.10 = (bf16[128,1024]{1,0:T(8,128)(2,1)S(1)}, bf16[128,1024]{1,0:T(8,128)(2,1)}, u32[]{:S(2)}) copy-start(bf16[128,1024]{1,0:T(8,128)(2,1)} %copy-done.9) | copy-start | bytes 786436
  355.2 43.2 %all-to-all-start.3 = ((bf16[128,2,2048]{2,0,1:T(8,128)(2,1)}), bf16[128,2,2048]{2,0,1:T(8,128)(2,1)S(1)}, u32[]{:S(2)}, u32[]{:S(2)}) async-start(bf16[128,2,2048]{2,0,1:T(8,128)(2,1)} %bitcast.87), calls=%async_computation.3 | async-start | bytes 2097152 | tf_op jit(solution)/shard_map/all_to_all | solution.py:188
  398.4 11.5 %all-to-all-start.2 = ((bf16[128,2,512]{2,0,1:T(8,128)(2,1)}), bf16[128,2,512]{2,0,1:T(8,128)(2,1)S(1)}, u32[]{:S(2)}, u32[]{:S(2)}) async-start(bf16[128,2,512]{2,0,1:T(8,128)(2,1)} %bitcast.88), calls=%async_computation.2 | async-start | bytes 524288 | tf_op jit(solution)/shard_map/all_to_all | solution.py:187
  401.9 247.5 %all-reduce.14.cloned.1.call-start = ((), (), s32[]{:S(2)}) async-start(), calls=%async_computation.9 | async-start | bytes 25165824 | tf_op jit(solution)/shard_map/psum | solution.py:256
  415.7 0.7 copy-start.31
  415.7 79.1 %copy-start.19 = (bf16[1,128,16,64]{1,3,2,0:T(8,128)(2,1)S(1)}, bf16[1,128,16,64]{1,3,2,0:T(8,128)(2,1)}, u32[]{:S(2)}) copy-start(bf16[1,128,16,64]{1,3,2,0:T(8,128)(2,1)} %get-tuple-element.115) | copy-start | bytes 786436
  415.7 79.1 %copy-start.20 = (bf16[16,64,128]{2,1,0:T(8,128)(2,1)S(1)}, bf16[16,64,128]{2,1,0:T(8,128)(2,1)}, u32[]{:S(2)}) copy-start(bf16[16,64,128]{2,1,0:T(8,128)(2,1)} %convolution_convert_fusion.4) | copy-start | bytes 786436
  415.7 79.1 %copy-start.21 = (bf16[1,128,16,64]{1,3,2,0:T(8,128)(2,1)S(1)}, bf16[1,128,16,64]{1,3,2,0:T(8,128)(2,1)}, u32[]{:S(2)}) copy-start(bf16[1,128,16,64]{1,3,2,0:T(8,128)(2,1)} %get-tuple-element.117) | copy-start | bytes 786436
  649.4 5.5 copy-start.7
  656.4 6.8 %copy-start.1 = (bf16[2048,1024]{1,0:T(8,128)(2,1)S(1)}, bf16[2048,1024]{1,0:T(8,128)(2,1)}, u32[]{:S(2)}) copy-start(bf16[2048,1024]{1,0:T(8,128)(2,1)} %get-tuple-element.104) | copy-start | bytes 12582916
Sparse Core Ops, SparseCore 0:
  9.5 150.5 all-gather.13
  161.7 33.3 all-gather.15
  196.7 103.9 all-gather.17
  333.1 32.3 all-gather.19
  366.8 43.9 all-gather.21
  416.4 232.9 all-reduce.13
